TPU v7x, 512 devices: a whole 4x8x8 slice. The times are simulated.
512 devices in a mesh: samp: 8 (over z), pair: 16 (over y_lo, x), recv: 4 (over y_hi, core).
Axes of the slice: x: 4, y: 8 (y_hi: 2, y_lo: 4; y = y_hi * 4 + y_lo), z: 8, core: 2. Of those that a mesh axis runs over, the one named last changes fastest.
Arguments:
- cell_expression: bfloat16 [32, 16384, 2048], P('samp', 'recv', 'pair'), may hold values from 0 to 24
- cell_labels: int32 [32, 16384], P('samp', 'recv'), may hold values from 0 to 127, as said below
- ligand_gene: int32 [2048], P('pair'), may hold values from 0 to 2047
- receptor_gene: int32 [2048], P('pair'), may hold values from 0 to 2047
- pair_factor: bfloat16 [2048, 32], P('pair'), may hold values from -0.53033009 to 0.53033009
- sender_factor: bfloat16 [128, 32], replicated, may hold values from -0.5 to 0.5
- receiver_factor: bfloat16 [128, 32], P('recv'), may hold values from -2.5 to 2.5
Outputs:
- sample_factor: float32 [32, 32], P('samp')
Inputs may be any that keep to these rules, and one draw needn't show every extreme that they name: `cell_labels`: in every sample one cell type has no cell.
All inputs are finite; a program needn't handle non-finite values.
Results may differ from a plain program's by a relative error of at most 0.0051.
Values may be sent and summed in bfloat16 or wider, within the bound.
No kernel may reach another device: no remote copies, remote signals or barrier semaphores. Data moves between devices by JAX's collectives and lax.ppermute only.
A program may use at most 64 MiB of HBM per device.

v0:
```python
import jax
import jax.numpy as jnp
from jax import lax
from jax.sharding import PartitionSpec as P


def body(
    cell_expression,
    cell_labels,
    ligand_gene,
    receptor_gene,
    pair_factor,
    sender_factor,
    receiver_factor,
):
    clusters = sender_factor.shape[0]
    factor_rank = sender_factor.shape[1]
    block_width = receiver_factor.shape[0]
    member = (
        cell_labels[:, :, None] == jnp.arange(clusters, dtype=jnp.int32)[None, None, :]
    ).astype(jnp.bfloat16)
    part_sums = jnp.einsum(
        "scg,sck->sgk", cell_expression, member, preferred_element_type=jnp.float32
    )
    part_counts = jnp.sum(member, axis=1, dtype=jnp.float32)
    receiver_start = lax.axis_index("recv") * block_width
    cluster_total, cell_count = lax.psum((part_sums, part_counts), "recv")
    cluster_mean = (cluster_total / jnp.maximum(cell_count, 1.0)[:, None, :]).astype(jnp.bfloat16)
    segment = lax.all_gather(cluster_mean, "pair", axis=1, tiled=True)
    ligand_table = jnp.einsum(
        "sga,ar->srg", segment, sender_factor, preferred_element_type=jnp.float32
    ).astype(jnp.bfloat16)
    receiver_columns = lax.dynamic_slice_in_dim(segment, receiver_start, block_width, 2)
    receptor_table = jnp.einsum(
        "sgb,br->srg", receiver_columns, receiver_factor, preferred_element_type=jnp.float32
    ).astype(jnp.bfloat16)
    joined_tables = jnp.concatenate([ligand_table, receptor_table], axis=1)
    ligand_rows = jnp.take(joined_tables[:, :factor_rank, :], ligand_gene, axis=2).astype(
        jnp.float32
    )
    receptor_rows = jnp.take(joined_tables[:, factor_rank:, :], receptor_gene, axis=2).astype(
        jnp.float32
    )
    pair_weights = pair_factor.astype(jnp.float32).T
    partial_product = jnp.sum(ligand_rows * receptor_rows * pair_weights[None, :, :], axis=2)
    pair_gram = jnp.einsum(
        "pr,pq->rq", pair_factor, pair_factor, preferred_element_type=jnp.float32
    )
    sender_gram = jnp.einsum(
        "pr,pq->rq", sender_factor, sender_factor, preferred_element_type=jnp.float32
    )
    receiver_gram = jnp.einsum(
        "pr,pq->rq", receiver_factor, receiver_factor, preferred_element_type=jnp.float32
    )
    product_total = lax.psum(partial_product, ("pair", "recv"))
    pair_gram = lax.psum(pair_gram, "pair")
    receiver_gram = lax.psum(receiver_gram, "recv")
    hadamard = pair_gram * sender_gram * receiver_gram
    cholesky_factor = jnp.linalg.cholesky(hadamard)
    solution = jax.scipy.linalg.cho_solve((cholesky_factor, True), product_total.T)
    return solution.T


def solution(mesh):
    placed = (
        P("samp", "recv", "pair"),
        P("samp", "recv"),
        P("pair"),
        P("pair"),
        P("pair", None),
        P(),
        P("recv", None),
    )
    return jax.shard_map(
        body, mesh=mesh, in_specs=placed, out_specs=P("samp", None), check_vma=False
    )
```

profile of v0, /device:TPU:9, one launch (start us, length us, event | category | flops | bytes accessed | tf_op | source)
XLA Modules:
  0.0 325.3 jit_solution(4889094992332328623)
XLA Ops:
  6.5 0.0 copy-start
  6.5 0.0 copy-start.2
  6.5 0.0 copy-start.3
  6.5 0.0 copy-start.1
  6.5 0.0 copy-start.4
  6.5 0.0 copy-start.5
  6.6 0.0 all-reduce.3.cloned.1.call-start
  6.6 4.6 %fusion.3 = f32[4,128,128]{1,2,0:T(8,128)} fusion(bf16[4,4096,128]{2,1,0:T(8,128)(2,1)} %param.9, s32[4,4096]{1,0:T(4,128)} %param.10), kind=kOutput, calls=%fused_computation.9 | convolution fusion | flops 538968064 | bytes 4521984 | tf_op jit(solution)/shard_map/scg,sck->sgk/dot_general | solution.py:22
  11.2 0.0 all-reduce.3.cloned.1.call-update
  11.2 0.0 all-gather.2.cloned.1.call-start
  11.3 0.0 copy-done.3
  11.3 0.2 fusion.16
  11.5 0.0 copy-done.2
  11.5 1.3 convert_reduce_fusion
  12.8 18.3 %all-reduce = (f32[4,128]{1,0:T(4,128)S(1)}, f32[32,32]{0,1:T(8,128)S(1)}) all-reduce(f32[4,128]{1,0:T(4,128)S(1)} %convert_reduce_fusion, f32[32,32]{0,1:T(8,128)S(1)} %fusion.16), channel_id=1, replica_groups=mesh['samp'=8,'pair'=16,'recv'=4] {'recv'}, use_global_device_ids=true, to_apply=%region_6.7 | all-reduce | flops 1536 | bytes 12288 | tf_op jit(solution)/shard_map/psum | solution.py:27
  31.0 43.7 %all-reduce.3.cloned.1.call-done = f32[4,128,128]{1,2,0:T(8,128)} async-done(((f32[4,128,128]{1,2,0:T(8,128)}), f32[4,128,128]{1,2,0:T(8,128)}) %all-reduce.3.cloned.1.call-update) | async-done | bytes 262160 | tf_op jit(solution)/shard_map/psum | solution.py:27
  74.7 1.7 divide_convert_fusion
  76.4 0.0 all-gather.2.cloned.1.call-update
  76.5 0.0 copy-done.1
  76.5 0.1 fusion.15
  76.6 57.9 %psum.35 = f32[32,32]{0,1:T(8,128)S(1)} all-reduce(f32[32,32]{0,1:T(8,128)S(1)} %fusion.15), channel_id=1, replica_groups=mesh['samp'=8,'pair'=16,'recv'=4] {'pair'}, use_global_device_ids=true, to_apply=%region_0.0 | all-reduce | flops 1024 | bytes 8192 | tf_op jit(solution)/shard_map/psum | solution.py:56
  134.5 0.0 copy-done
  134.5 0.1 fusion.4
  134.6 0.1 copy.16
  134.7 2.9 cholesky.16
  137.6 0.6 compare_reduce_fusion
  138.3 0.7 fusion.6
  138.9 2.5 custom-call.10
  141.4 0.1 copy.17
  141.5 0.0 copy-done.4
  141.5 0.0 copy-done.5
  141.6 0.3 all-gather.2.cloned.1.call-done
  141.8 2.0 convolution_convert_fusion
  143.8 1.4 copy.23
  145.2 1.4 convolution_convert_fusion.1
  146.6 2.5 copy.24
  149.1 0.7 gather_fusion
  149.9 2.3 gather_fusion.1
  152.2 0.3 multiply_reduce_fusion
  152.6 164.9 %psum.39 = f32[4,32]{1,0:T(4,128)S(1)} all-reduce(f32[4,32]{1,0:T(4,128)S(1)} %multiply_reduce_fusion), channel_id=1, replica_groups=mesh['samp'=8,'pair'=16,'recv'=4] {'pair','recv'}, use_global_device_ids=true, to_apply=%region_8.10 | all-reduce | flops 128 | bytes 1024 | tf_op jit(solution)/shard_map/psum | solution.py:55
  317.5 0.2 fusion.9
  317.7 0.8 fusion.7
  (9 shorter events, 0.1 us)
Async XLA Ops:
  6.5 127.9 %copy-start = (bf16[128,32]{0,1:T(8,128)(2,1)S(1)}, bf16[128,32]{0,1:T(8,128)(2,1)}, u32[]{:S(2)}) copy-start(bf16[128,32]{0,1:T(8,128)(2,1)} %param.14) | copy-start | bytes 24580
  6.5 4.9 %copy-start.2 = (s32[4,4096]{1,0:T(4,128)S(1)}, s32[4,4096]{1,0:T(4,128)}, u32[]{:S(2)}) copy-start(s32[4,4096]{1,0:T(4,128)} %param.10) | copy-start | bytes 196612
  6.5 4.7 %copy-start.3 = (bf16[32,32]{1,0:T(8,128)(2,1)S(1)}, bf16[32,32]{1,0:T(8,128)(2,1)}, u32[]{:S(2)}) copy-start(bf16[32,32]{1,0:T(8,128)(2,1)} %param.15) | copy-start | bytes 6148
  6.5 69.9 %copy-start.1 = (bf16[128,32]{0,1:T(8,128)(2,1)S(1)}, bf16[128,32]{0,1:T(8,128)(2,1)}, u32[]{:S(2)}) copy-start(bf16[128,32]{0,1:T(8,128)(2,1)} %param.13) | copy-start | bytes 24580
  6.5 134.9 %copy-start.4 = (s32[128]{0:T(128)S(1)}, s32[128]{0:T(128)}, u32[]{:S(2)}) copy-start(s32[128]{0:T(128)} %param.12) | copy-start | bytes 1540
  6.5 135.0 %copy-start.5 = (s32[128]{0:T(128)S(1)}, s32[128]{0:T(128)}, u32[]{:S(2)}) copy-start(s32[128]{0:T(128)} %param.11) | copy-start | bytes 1540
  6.6 68.1 %all-reduce.3.cloned.1.call-start = ((), (), s32[]{:S(2)}) async-start(), calls=%async_computation | async-start | bytes 524288 | tf_op jit(solution)/shard_map/psum | solution.py:27
  11.2 130.6 %all-gather.2.cloned.1.call-start = ((), (), s32[]{:S(2)}) async-start(), calls=%async_computation.1 | async-start | bytes 2228224 | tf_op jit(solution)/shard_map/all_gather | solution.py:29
Sparse Core Ops, SparseCore 0:
  11.3 63.2 all-reduce.2
  76.9 64.9 all-gather.1
where the time goes:
time: 326 us; the launch traced here: 325 us
  blocking collectives  241 us (74%)
  waiting for transfers between devices  43.9 us (13%)
  between operations  13.6 us (4%)
  other arithmetic  10.1 us (3%)
  matrix products  9.4 us (3%)
  local copies, waits for them, and re-layouts  7.17 us (2%)
    psum x1, blocking collectives, body(): product_total = lax.psum(partial_product, ('pair', 'recv'))  165 us
    psum x1, blocking collectives, body(): pair_gram = lax.psum(pair_gram, 'pair')  57.9 us
    psum x1, waiting for transfers between devices, body(): cluster_total, cell_count = lax.psum((part_sums, part_counts), 'recv')  43.7 us
    psum x1, blocking collectives, body(): cluster_total, cell_count = lax.psum((part_sums, part_counts), 'recv')  18.3 us
  transfers between devices with their start and end apart: 2, of which 2 were waited for; matrix products, arithmetic and copies ran while one was open for 3% of the time, Pallas kernels for 0%

commit v1 on v0

--- a/solution.py
+++ b/solution.py
@@ -53,7 +53,7 @@
         "pr,pq->rq", receiver_factor, receiver_factor, preferred_element_type=jnp.float32
     )
     product_total = lax.psum(partial_product, ("pair", "recv"))
-    pair_gram = lax.psum(pair_gram, "pair")
+    pair_gram = jnp.sum(lax.all_gather(pair_gram, "pair"), axis=0)
     receiver_gram = lax.psum(receiver_gram, "recv")
     hadamard = pair_gram * sender_gram * receiver_gram
     cholesky_factor = jnp.linalg.cholesky(hadamard)

time: 326 us -> 323 us (level)
  the two profiles are of different devices: /device:TPU:9 before, /device:TPU:24 now
where the time goes in v1:
time: 323 us
  blocking collectives  208 us (64%)
  waiting for transfers between devices  74.4 us (23%)
  between operations  13.6 us (4%)
  other arithmetic  10.2 us (3%)
  matrix products  9.26 us (3%)
  local copies, waits for them, and re-layouts  7.24 us (2%)
    psum x1, blocking collectives, body(): product_total = lax.psum(partial_product, ('pair', 'recv'))  153 us
    psum x1, waiting for transfers between devices, body(): cluster_total, cell_count = lax.psum((part_sums, part_counts), 'recv')  38.7 us
    all_gather x1, waiting for transfers between devices, body(): segment = lax.all_gather(cluster_mean, 'pair', axis=1, tiled=True)  35.7 us
    all_gather x1, blocking collectives, body(): pair_gram = jnp.sum(lax.all_gather(pair_gram, 'pair'), axis=0)  34.7 us
    psum x1, blocking collectives, body(): cluster_total, cell_count = lax.psum((part_sums, part_counts), 'recv')  20.8 us
  transfers between devices with their start and end apart: 2, of which 2 were waited for; matrix products, arithmetic and copies ran while one was open for 3% of the time, Pallas kernels for 0%

profile of v1, /device:TPU:24, one launch (start us, length us, event | category | flops | bytes accessed | tf_op | source)
XLA Modules:
  0.0 323.1 jit_solution(1918330318000444838)
XLA Ops:
  6.5 0.0 copy-start
  6.5 0.0 copy-start.2
  6.5 0.0 copy-start.3
  6.5 0.0 copy-start.1
  6.5 0.0 copy-start.4
  6.5 0.0 copy-start.5
  6.6 0.0 all-reduce.3.cloned.1.call-start
  6.6 4.6 %fusion.5 = f32[4,128,128]{1,2,0:T(8,128)} fusion(bf16[4,4096,128]{2,1,0:T(8,128)(2,1)} %param.9, s32[4,4096]{1,0:T(4,128)} %param.10), kind=kOutput, calls=%fused_computation.11 | convolution fusion | flops 538968064 | bytes 4521984 | tf_op jit(solution)/shard_map/scg,sck->sgk/dot_general | solution.py:22
  11.2 0.0 all-reduce.3.cloned.1.call-update
  11.2 0.0 all-gather.3.cloned.1.call-start
  11.3 0.0 copy-done.3
  11.3 0.2 fusion.18
  11.5 0.0 copy-done.2
  11.5 1.3 convert_reduce_fusion
  12.8 20.8 %all-reduce = (f32[4,128]{1,0:T(4,128)S(1)}, f32[32,32]{0,1:T(8,128)S(1)}) all-reduce(f32[4,128]{1,0:T(4,128)S(1)} %convert_reduce_fusion, f32[32,32]{0,1:T(8,128)S(1)} %fusion.18), channel_id=1, replica_groups=mesh['samp'=8,'pair'=16,'recv'=4] {'recv'}, use_global_device_ids=true, to_apply=%region_6.7 | all-reduce | flops 1536 | bytes 12288 | tf_op jit(solution)/shard_map/psum | solution.py:27
  33.6 38.7 %all-reduce.3.cloned.1.call-done = f32[4,128,128]{1,2,0:T(8,128)} async-done(((f32[4,128,128]{1,2,0:T(8,128)}), f32[4,128,128]{1,2,0:T(8,128)}) %all-reduce.3.cloned.1.call-update) | async-done | bytes 262160 | tf_op jit(solution)/shard_map/psum | solution.py:27
  72.3 1.7 divide_convert_fusion
  74.0 0.0 all-gather.3.cloned.1.call-update
  74.1 0.0 copy-done.1
  74.1 0.1 copy.24
  74.2 0.1 fusion.17
  74.3 34.7 %all-gather = f32[512,32]{1,0:T(8,128)S(1)} all-gather(f32[32,32]{1,0:T(8,128)S(1)} %fusion.17), channel_id=2, replica_groups=mesh['samp'=8,'pair'=16,'recv'=4] {'pair'}, dimensions={0}, use_global_device_ids=true | all-gather | bytes 69632 | tf_op jit(solution)/shard_map/all_gather | solution.py:56
  109.0 0.1 copy.16
  109.1 0.0 copy-done
  109.1 0.1 fusion.6
  109.2 0.1 copy.19
  109.3 2.9 cholesky.16
  112.3 0.6 compare_reduce_fusion
  112.9 0.7 fusion.8
  113.6 2.5 custom-call.10
  116.0 0.0 copy-done.4
  116.1 0.0 copy-done.5
  116.1 35.7 %all-gather.3.cloned.1.call-done = bf16[4,2048,128]{1,2,0:T(8,128)(2,1)} async-done(((bf16[4,128,128]{1,2,0:T(8,128)(2,1)}), bf16[4,2048,128]{1,2,0:T(8,128)(2,1)}) %all-gather.3.cloned.1.call-update) | async-done | bytes 2097168 | tf_op jit(solution)/shard_map/all_gather | solution.py:29
  151.8 2.0 fusion.3
  153.8 1.4 copy.21
  155.2 1.4 fusion.4
  156.6 2.5 copy.23
  159.1 0.7 gather_fusion
  159.8 2.3 gather_fusion.1
  162.2 0.3 multiply_reduce_fusion
  162.5 152.9 %psum.31 = f32[4,32]{1,0:T(4,128)S(1)} all-reduce(f32[4,32]{1,0:T(4,128)S(1)} %multiply_reduce_fusion), channel_id=1, replica_groups=mesh['samp'=8,'pair'=16,'recv'=4] {'pair','recv'}, use_global_device_ids=true, to_apply=%region_8.10 | all-reduce | flops 128 | bytes 1024 | tf_op jit(solution)/shard_map/psum | solution.py:55
  315.4 0.1 fusion.11
  315.5 0.7 fusion.9
  (10 shorter events, 0.1 us)
Async XLA Ops:
  6.5 102.6 %copy-start = (bf16[128,32]{0,1:T(8,128)(2,1)S(1)}, bf16[128,32]{0,1:T(8,128)(2,1)}, u32[]{:S(2)}) copy-start(bf16[128,32]{0,1:T(8,128)(2,1)} %param.14) | copy-start | bytes 24580
  6.5 4.9 %copy-start.2 = (s32[4,4096]{1,0:T(4,128)S(1)}, s32[4,4096]{1,0:T(4,128)}, u32[]{:S(2)}) copy-start(s32[4,4096]{1,0:T(4,128)} %param.10) | copy-start | bytes 196612
  6.5 4.7 %copy-start.3 = (bf16[32,32]{1,0:T(8,128)(2,1)S(1)}, bf16[32,32]{1,0:T(8,128)(2,1)}, u32[]{:S(2)}) copy-start(bf16[32,32]{1,0:T(8,128)(2,1)} %param.15) | copy-start | bytes 6148
  6.5 67.5 %copy-start.1 = (bf16[128,32]{0,1:T(8,128)(2,1)S(1)}, bf16[128,32]{0,1:T(8,128)(2,1)}, u32[]{:S(2)}) copy-start(bf16[128,32]{0,1:T(8,128)(2,1)} %param.13) | copy-start | bytes 24580
  6.5 109.5 %copy-start.4 = (s32[128]{0:T(128)S(1)}, s32[128]{0:T(128)}, u32[]{:S(2)}) copy-start(s32[128]{0:T(128)} %param.12) | copy-start | bytes 1540
  6.5 109.5 %copy-start.5 = (s32[128]{0:T(128)S(1)}, s32[128]{0:T(128)}, u32[]{:S(2)}) copy-start(s32[128]{0:T(128)} %param.11) | copy-start | bytes 1540
  6.6 65.7 %all-reduce.3.cloned.1.call-start = ((), (), s32[]{:S(2)}) async-start(), calls=%async_computation | async-start | bytes 524288 | tf_op jit(solution)/shard_map/psum | solution.py:27
  11.2 140.6 %all-gather.3.cloned.1.call-start = ((), (), s32[]{:S(2)}) async-start(), calls=%async_computation.1 | async-start | bytes 2228224 | tf_op jit(solution)/shard_map/all_gather | solution.py:29
Sparse Core Ops, SparseCore 0:
  11.4 60.8 all-reduce.2
  74.5 77.2 all-gather.2

commit v2 on v0

--- a/solution.py
+++ b/solution.py
@@ -52,7 +52,7 @@
     receiver_gram = jnp.einsum(
         "pr,pq->rq", receiver_factor, receiver_factor, preferred_element_type=jnp.float32
     )
-    product_total = lax.psum(partial_product, ("pair", "recv"))
+    product_total = lax.psum(lax.psum(partial_product, "recv"), "pair")
     pair_gram = lax.psum(pair_gram, "pair")
     receiver_gram = lax.psum(receiver_gram, "recv")
     hadamard = pair_gram * sender_gram * receiver_gram

time: 326 us -> 273 us (0.84)
  the two profiles are of different devices: /device:TPU:9 before, /device:TPU:64 now
where the time goes in v2:
time: 273 us
  waiting for transfers between devices  120 us (44%)
  blocking collectives  113 us (41%)
  between operations  13.6 us (5%)
  other arithmetic  10.1 us (4%)
  matrix products  9.45 us (3%)
  local copies, waits for them, and re-layouts  7.16 us (3%)
    psum x2, blocking collectives, body(): product_total = lax.psum(lax.psum(partial_product, 'recv'), 'pair')  97.5 us
    all_gather x1, waiting for transfers between devices, body(): segment = lax.all_gather(cluster_mean, 'pair', axis=1, tiled=True)  72.8 us
    psum x1, waiting for transfers between devices, body(): cluster_total, cell_count = lax.psum((part_sums, part_counts), 'recv')  47 us
    psum x1, blocking collectives, body(): cluster_total, cell_count = lax.psum((part_sums, part_counts), 'recv')  15.1 us
  transfers between devices with their start and end apart: 2, of which 2 were waited for; matrix products, arithmetic and copies ran while one was open for 1% of the time, Pallas kernels for 0%

profile of v2, /device:TPU:64, one launch (start us, length us, event | category | flops | bytes accessed | tf_op | source)
XLA Modules:
  0.0 272.8 jit_solution(14452679809832513594)
XLA Ops:
  6.5 0.0 copy-start
  6.5 0.0 copy-start.3
  6.5 0.0 copy-start.2
  6.5 0.0 copy-start.4
  6.5 0.0 copy-start.5
  6.5 0.0 copy-start.1
  6.6 0.0 all-reduce.4.cloned.1.call-start
  6.6 4.6 %fusion.3 = f32[4,128,128]{1,2,0:T(8,128)} fusion(bf16[4,4096,128]{2,1,0:T(8,128)(2,1)} %param.9, s32[4,4096]{1,0:T(4,128)} %param.10), kind=kOutput, calls=%fused_computation.9 | convolution fusion | flops 538968064 | bytes 4521984 | tf_op jit(solution)/shard_map/scg,sck->sgk/dot_general | solution.py:22
  11.2 0.0 all-reduce.4.cloned.1.call-update
  11.2 0.0 all-gather.2.cloned.1.call-start
  11.3 0.0 copy-done.3
  11.3 1.3 convert_reduce_fusion
  12.6 15.1 %psum.45 = f32[4,128]{1,0:T(4,128)S(1)} all-reduce(f32[4,128]{1,0:T(4,128)S(1)} %convert_reduce_fusion), channel_id=1, replica_groups=mesh['samp'=8,'pair'=16,'recv'=4] {'recv'}, use_global_device_ids=true, to_apply=%region_6.7 | all-reduce | flops 512 | bytes 4096 | tf_op jit(solution)/shard_map/psum | solution.py:27
  27.7 47.0 %all-reduce.4.cloned.1.call-done = f32[4,128,128]{1,2,0:T(8,128)} async-done(((f32[4,128,128]{1,2,0:T(8,128)}), f32[4,128,128]{1,2,0:T(8,128)}) %all-reduce.4.cloned.1.call-update) | async-done | bytes 262160 | tf_op jit(solution)/shard_map/psum | solution.py:27
  74.7 1.7 divide_convert_fusion
  76.4 0.0 all-gather.2.cloned.1.call-update
  76.5 0.0 copy-done.2
  76.5 0.1 copy.17
  76.6 0.0 copy-done.4
  76.6 0.0 copy-done.5
  76.7 0.1 fusion.15
  76.8 0.0 copy-done
  76.8 0.2 fusion.16
  77.0 72.8 %all-gather.2.cloned.1.call-done = bf16[4,2048,128]{1,2,0:T(8,128)(2,1)} async-done(((bf16[4,128,128]{1,2,0:T(8,128)(2,1)}), bf16[4,2048,128]{1,2,0:T(8,128)(2,1)}) %all-gather.2.cloned.1.call-update) | async-done | bytes 2097168 | tf_op jit(solution)/shard_map/all_gather | solution.py:29
  149.8 0.0 copy-done.1
  149.8 2.0 convolution_convert_fusion
  151.8 1.4 copy.23
  153.2 1.4 convolution_convert_fusion.1
  154.6 2.5 copy.24
  157.1 0.7 gather_fusion
  157.8 2.3 gather_fusion.1
  160.2 0.3 multiply_reduce_fusion
  160.5 18.1 %all-reduce.1 = (f32[4,32]{1,0:T(4,128)S(1)}, f32[32,32]{0,1:T(8,128)S(1)}) all-reduce(f32[4,32]{1,0:T(4,128)S(1)} %multiply_reduce_fusion, f32[32,32]{0,1:T(8,128)S(1)} %fusion.16), channel_id=1, replica_groups=mesh['samp'=8,'pair'=16,'recv'=4] {'recv'}, use_global_device_ids=true, to_apply=%region_8.10 | all-reduce | flops 1152 | bytes 9216 | tf_op jit(solution)/shard_map/psum | solution.py:55
  178.6 79.5 %all-reduce = (f32[4,32]{1,0:T(4,128)S(1)}, f32[32,32]{0,1:T(8,128)S(1)}) all-reduce(f32[4,32]{1,0:T(4,128)S(1)} %get-tuple-element.8, f32[32,32]{0,1:T(8,128)S(1)} %fusion.15), channel_id=1, replica_groups=mesh['samp'=8,'pair'=16,'recv'=4] {'pair'}, use_global_device_ids=true, to_apply=%region_9.11 | all-reduce | flops 1152 | bytes 9216 | tf_op jit(solution)/shard_map/psum | solution.py:55
  258.1 0.1 fusion.4
  258.2 0.1 copy.16
  258.3 2.9 %cholesky.16 = f32[32,32]{1,0:T(8,128)S(1)} custom-call(f32[32,32]{1,0:T(8,128)S(1)} %fusion.11), custom_call_target="Cholesky" | custom-call | tf_op jit(solution)/shard_map/jit(cholesky)/cholesky | solution.py:59
  261.2 0.6 compare_reduce_fusion
  261.9 0.7 fusion.6
  262.5 2.4 custom-call.10
  265.0 0.2 fusion.9
  265.2 0.8 fusion.7
  (9 shorter events, 0.1 us)
Async XLA Ops:
  6.5 70.3 %copy-start = (bf16[32,32]{1,0:T(8,128)(2,1)S(1)}, bf16[32,32]{1,0:T(8,128)(2,1)}, u32[]{:S(2)}) copy-start(bf16[32,32]{1,0:T(8,128)(2,1)} %param.15) | copy-start | bytes 6148
  6.5 4.8 %copy-start.3 = (s32[4,4096]{1,0:T(4,128)S(1)}, s32[4,4096]{1,0:T(4,128)}, u32[]{:S(2)}) copy-start(s32[4,4096]{1,0:T(4,128)} %param.10) | copy-start | bytes 196612
  6.5 69.9 %copy-start.2 = (bf16[128,32]{0,1:T(8,128)(2,1)S(1)}, bf16[128,32]{0,1:T(8,128)(2,1)}, u32[]{:S(2)}) copy-start(bf16[128,32]{0,1:T(8,128)(2,1)} %param.13) | copy-start | bytes 24580
  6.5 70.0 %copy-start.4 = (s32[128]{0:T(128)S(1)}, s32[128]{0:T(128)}, u32[]{:S(2)}) copy-start(s32[128]{0:T(128)} %param.12) | copy-start | bytes 1540
  6.5 70.1 %copy-start.5 = (s32[128]{0:T(128)S(1)}, s32[128]{0:T(128)}, u32[]{:S(2)}) copy-start(s32[128]{0:T(128)} %param.11) | copy-start | bytes 1540
  6.5 143.3 %copy-start.1 = (bf16[128,32]{0,1:T(8,128)(2,1)S(1)}, bf16[128,32]{0,1:T(8,128)(2,1)}, u32[]{:S(2)}) copy-start(bf16[128,32]{0,1:T(8,128)(2,1)} %param.14) | copy-start | bytes 24580
  6.6 68.1 %all-reduce.4.cloned.1.call-start = ((), (), s32[]{:S(2)}) async-start(), calls=%async_computation | async-start | bytes 524288 | tf_op jit(solution)/shard_map/psum | solution.py:27
  11.2 138.6 %all-gather.2.cloned.1.call-start = ((), (), s32[]{:S(2)}) async-start(), calls=%async_computation.1 | async-start | bytes 2228224 | tf_op jit(solution)/shard_map/all_gather | solution.py:29
Sparse Core Ops, SparseCore 0:
  11.4 63.2 all-reduce.3
  76.9 72.8 all-gather.1
